TPU v7x, 32 devices: a whole 2x2x4 slice. The times are simulated.
32 devices in a mesh: dp: 8 (over y, x, core), mp: 4 (over z).
Axes of the slice: x: 2, y: 2, z: 4, core: 2. Of those that a mesh axis runs over, the one named last changes fastest.
Arguments:
- tokens_in: bfloat16 [8192, 2048], P('dp'), may hold values from -6 to 6
- cotangent: bfloat16 [8192, 2048], P('dp'), may hold values from -6 to 6
- seq_lengths: int32 [8, 4], P('dp'), may hold values from 0 to 512, as said below
- qkv_weight: bfloat16 [2, 2048, 6144], P(None, 'dp', 'mp'), may hold values from -0.125 to 0.125
- dense_weight: bfloat16 [2, 2048, 2048], P(None, 'mp', 'dp'), may hold values from -0.5 to 0.5
- up_weight: bfloat16 [2, 2048, 8192], P(None, 'dp', 'mp'), may hold values from -0.125 to 0.125
- down_weight: bfloat16 [2, 8192, 2048], P(None, 'mp', 'dp'), may hold values from -0.0625 to 0.0625
- qkv_bias: bfloat16 [2, 48, 128], P(None, 'mp', 'dp'), may hold values from -3 to 3
- up_bias: bfloat16 [2, 64, 128], P(None, 'mp', 'dp'), may hold values from -3 to 3
- vectors: bfloat16 [2, 6, 2048], P(None, None, 'dp')
- qkv_weight_first: float32 [2, 2048, 6144], P(None, 'dp', 'mp'), may hold values from -96 to 96
- dense_weight_first: float32 [2, 2048, 2048], P(None, 'mp', 'dp'), may hold values from -48 to 48
- up_weight_first: float32 [2, 2048, 8192], P(None, 'dp', 'mp'), may hold values from -16 to 16
- down_weight_first: float32 [2, 8192, 2048], P(None, 'mp', 'dp'), may hold values from -40 to 40
- qkv_bias_first: float32 [2, 48, 128], P(None, 'mp', 'dp'), may hold values from -128 to 128
- up_bias_first: float32 [2, 64, 128], P(None, 'mp', 'dp'), may hold values from -16 to 16
- vectors_first: float32 [2, 6, 2048], P(None, None, 'dp'), may hold values from -128 to 128
- qkv_weight_second: float32 [2, 2048, 6144], P(None, 'dp', 'mp'), may hold values from 1720.32 to 6799.36
- dense_weight_second: float32 [2, 2048, 2048], P(None, 'mp', 'dp'), may hold values from 450.56 to 1802.24
- up_weight_second: float32 [2, 2048, 8192], P(None, 'dp', 'mp'), may hold values from 61.44 to 245.76
- down_weight_second: float32 [2, 8192, 2048], P(None, 'mp', 'dp'), may hold values from 327.68 to 1310.72
- qkv_bias_second: float32 [2, 48, 128], P(None, 'mp', 'dp'), may hold values from 4096 to 16384
- up_bias_second: float32 [2, 64, 128], P(None, 'mp', 'dp'), may hold values from 39.3216 to 155.648
- vectors_second: float32 [2, 6, 2048], P(None, None, 'dp'), may hold values from 2293.76 to 9256.96
Outputs:
- block_output: bfloat16 [8192, 2048], P('dp')
- input_grad: float32 [8192, 2048], P('dp')
- qkv_weight_grad: float32 [2, 2048, 6144], P(None, 'dp', 'mp')
- qkv_weight_first_new: float32 [2, 2048, 6144], P(None, 'dp', 'mp')
- qkv_weight_second_new: float32 [2, 2048, 6144], P(None, 'dp', 'mp')
- qkv_weight_step: float32 [2, 2048, 6144], P(None, 'dp', 'mp')
- dense_weight_grad: float32 [2, 2048, 2048], P(None, 'mp', 'dp')
- dense_weight_first_new: float32 [2, 2048, 2048], P(None, 'mp', 'dp')
- dense_weight_second_new: float32 [2, 2048, 2048], P(None, 'mp', 'dp')
- dense_weight_step: float32 [2, 2048, 2048], P(None, 'mp', 'dp')
- up_weight_grad: float32 [2, 2048, 8192], P(None, 'dp', 'mp')
- up_weight_first_new: float32 [2, 2048, 8192], P(None, 'dp', 'mp')
- up_weight_second_new: float32 [2, 2048, 8192], P(None, 'dp', 'mp')
- up_weight_step: float32 [2, 2048, 8192], P(None, 'dp', 'mp')
- down_weight_grad: float32 [2, 8192, 2048], P(None, 'mp', 'dp')
- down_weight_first_new: float32 [2, 8192, 2048], P(None, 'mp', 'dp')
- down_weight_second_new: float32 [2, 8192, 2048], P(None, 'mp', 'dp')
- down_weight_step: float32 [2, 8192, 2048], P(None, 'mp', 'dp')
- qkv_bias_grad: float32 [2, 48, 128], P(None, 'mp', 'dp')
- qkv_bias_first_new: float32 [2, 48, 128], P(None, 'mp', 'dp')
- qkv_bias_second_new: float32 [2, 48, 128], P(None, 'mp', 'dp')
- qkv_bias_step: float32 [2, 48, 128], P(None, 'mp', 'dp')
- up_bias_grad: float32 [2, 64, 128], P(None, 'mp', 'dp')
- up_bias_first_new: float32 [2, 64, 128], P(None, 'mp', 'dp')
- up_bias_second_new: float32 [2, 64, 128], P(None, 'mp', 'dp')
- up_bias_step: float32 [2, 64, 128], P(None, 'mp', 'dp')
- vectors_grad: float32 [2, 6, 2048], P(None, None, 'dp')
- updated_vector_first_moment: float32 [2, 6, 2048], P(None, None, 'dp')
- vectors_second_new: float32 [2, 6, 2048], P(None, None, 'dp')
- vectors_step: float32 [2, 6, 2048], P(None, None, 'dp')
Inputs may be any that keep to these rules, and one draw needn't show every extreme that they name: `seq_lengths`: A zero marks an empty slot; the lengths of one index of dp sum to at most 1024, and in every draw some index of dp sums to exactly 1024 with sequences of 512; any other length lies between 64 and 512.
All inputs are finite; a program needn't handle non-finite values.
Results may differ from a plain program's by a relative error of at most 0.012.
Values may be sent and summed in bfloat16 or wider, within the bound.
A program may use at most 384 MiB of HBM per device.

v0:
```python
import jax
import jax.numpy as jnp
from jax import lax
from jax.sharding import PartitionSpec as P

HD = 256
ROT = 64
LAYERS = 2
MAXLEN = 512
ADAM_STEP = 10
norm_eps = 1e-05
beta_one = 0.9
beta_two = 0.95
adam_eps = 1e-08
rate = 0.02
decay = 0.01
masked_score = -1e30


def layout(lengths_row, rows):
    slots = lengths_row.shape[0]
    ends = jnp.cumsum(lengths_row)
    starts = ends - lengths_row
    index = jnp.arange(rows, dtype=jnp.int32)
    inside = (index[:, None] >= starts[None, :]) & (index[:, None] < ends[None, :])
    valid = jnp.any(inside, axis=1)
    number = jnp.arange(slots, dtype=jnp.int32)
    slot = jnp.sum(jnp.where(inside, number[None, :], 0), axis=1)
    first = jnp.sum(jnp.where(inside, starts[None, :], 0), axis=1)
    segment = jnp.where(valid, slot, slots + index)
    position = index - first
    return (segment, position, valid)


def rotary_tables(position):
    half = ROT // 2
    freq = 10000.0 ** (-(jnp.arange(half, dtype=jnp.float32) * 2.0) / ROT)
    angle = position.astype(jnp.float32)[:, None] * freq[None, :]
    return (jnp.cos(angle), jnp.sin(angle))


def rotate(values, cosine, sine):
    half = cosine.shape[1]
    first = values[..., :half]
    second = values[..., half : 2 * half]
    rest = values[..., 2 * half :]
    cfac = cosine[:, None, :]
    sfac = sine[:, None, :]
    return jnp.concatenate(
        [first * cfac - second * sfac, second * cfac + first * sfac, rest], axis=-1
    )


def apply_layer_norm(residual_stream):
    centre = jnp.mean(residual_stream, axis=1, keepdims=True)
    centred = residual_stream - centre
    spread = jnp.mean(centred * centred, axis=1, keepdims=True)
    return centred * lax.rsqrt(spread + norm_eps)


def norm_pair(residual_stream, model_parameters):
    normalized_input_rows = apply_layer_norm(residual_stream)
    return (
        normalized_input_rows * model_parameters[0] + model_parameters[1],
        normalized_input_rows * model_parameters[2] + model_parameters[3],
    )


def gelu_exact(values):
    return jax.nn.gelu(values, approximate=False)


def padded_inputs(keys, values, segment):
    block = MAXLEN
    rows, heads, width = keys.shape
    zeros = jnp.zeros((block, heads, width), keys.dtype)
    keys_pad = jnp.concatenate([zeros, keys], axis=0)
    values_pad = jnp.concatenate([zeros, values], axis=0)
    seg_pad = jnp.concatenate([jnp.full((block,), -1, jnp.int32), segment])
    padded_index_rows = jnp.arange(-block, rows, dtype=jnp.int32)
    return (keys_pad, values_pad, seg_pad, padded_index_rows)


def window(query, keys_pad, values_pad, seg_pad, padded_index_rows, segment, number):
    block = MAXLEN
    start = number * block
    q_blk = lax.dynamic_slice_in_dim(query, start, block, 0)
    k_win = lax.dynamic_slice_in_dim(keys_pad, start, 2 * block, 0)
    v_win = lax.dynamic_slice_in_dim(values_pad, start, 2 * block, 0)
    seg_q = lax.dynamic_slice_in_dim(segment, start, block, 0)
    seg_k = lax.dynamic_slice_in_dim(seg_pad, start, 2 * block, 0)
    idx_q = start + jnp.arange(block, dtype=jnp.int32)
    idx_k = lax.dynamic_slice_in_dim(padded_index_rows, start, 2 * block, 0)
    allowed = (seg_q[:, None] == seg_k[None, :]) & (idx_k[None, :] <= idx_q[:, None])
    scores = jnp.einsum("qhd,khd->hqk", q_blk, k_win, preferred_element_type=jnp.float32) * HD ** (
        -0.5
    )
    scores = jnp.where(allowed[None], scores, masked_score)
    return (start, q_blk, k_win, v_win, scores)


def attention_forward(query, keys, values, segment):
    rows, heads, width = query.shape
    count = rows // MAXLEN
    keys_pad, values_pad, seg_pad, padded_index_rows = padded_inputs(keys, values, segment)

    def one_block(number):
        start, q_blk, k_win, v_win, scores = window(
            query, keys_pad, values_pad, seg_pad, padded_index_rows, segment, number
        )
        top = jnp.max(scores, axis=2, keepdims=True)
        expo = jnp.exp(scores - top)
        total = jnp.sum(expo, axis=2, keepdims=True)
        prob = (expo / total).astype(jnp.bfloat16)
        context = jnp.einsum("hqk,khd->qhd", prob, v_win, preferred_element_type=jnp.float32)
        return (context.astype(jnp.bfloat16), (top + jnp.log(total))[:, :, 0])

    context, logsum = lax.map(one_block, jnp.arange(count, dtype=jnp.int32))
    return (context.reshape(rows, heads * width), logsum)


def attention_backward(query, keys, values, d_context, logsum, segment):
    rows, heads, width = query.shape
    block = MAXLEN
    count = rows // block
    keys_pad, values_pad, seg_pad, padded_index_rows = padded_inputs(keys, values, segment)

    def one_block(carry, inputs):
        dk_acc, dv_acc = carry
        number, lse_blk = inputs
        start, q_blk, k_win, v_win, scores = window(
            query, keys_pad, values_pad, seg_pad, padded_index_rows, segment, number
        )
        do_blk = lax.dynamic_slice_in_dim(d_context, start, block, 0)
        prob = jnp.exp(scores - lse_blk[:, :, None])
        d_prob = jnp.einsum("qhd,khd->hqk", do_blk, v_win, preferred_element_type=jnp.float32)
        delta = jnp.sum(prob * d_prob, axis=2, keepdims=True)
        d_score = (prob * (d_prob - delta)).astype(jnp.bfloat16)
        d_query = jnp.einsum(
            "hqk,khd->qhd", d_score, k_win, preferred_element_type=jnp.float32
        ) * HD ** (-0.5)
        d_keys = jnp.einsum(
            "hqk,qhd->khd", d_score, q_blk, preferred_element_type=jnp.float32
        ) * HD ** (-0.5)
        d_values = jnp.einsum(
            "hqk,qhd->khd", prob.astype(jnp.bfloat16), do_blk, preferred_element_type=jnp.float32
        )
        dk_acc = lax.dynamic_update_slice_in_dim(
            dk_acc, lax.dynamic_slice_in_dim(dk_acc, start, 2 * block, 0) + d_keys, start, 0
        )
        dv_acc = lax.dynamic_update_slice_in_dim(
            dv_acc, lax.dynamic_slice_in_dim(dv_acc, start, 2 * block, 0) + d_values, start, 0
        )
        return ((dk_acc, dv_acc), d_query)

    empty = jnp.zeros((rows + block, heads, width), jnp.float32)
    (dk_acc, dv_acc), d_query = lax.scan(
        one_block, (empty, empty), (jnp.arange(count, dtype=jnp.int32), logsum)
    )
    return (d_query.reshape(rows, heads, width), dk_acc[block:], dv_acc[block:])


def fetch(shards, layer):
    return (
        lax.all_gather(shards[0][layer], "dp", axis=0, tiled=True),
        lax.all_gather(shards[1][layer], "dp", axis=1, tiled=True),
        lax.all_gather(shards[2][layer], "dp", axis=0, tiled=True),
        lax.all_gather(shards[3][layer], "dp", axis=1, tiled=True),
        lax.all_gather(shards[4][layer], "dp", axis=1, tiled=True),
        lax.all_gather(shards[5][layer], "dp", axis=1, tiled=True),
        lax.all_gather(shards[6][layer], "dp", axis=1, tiled=True),
    )


def reduce_grads(grads):
    return (
        lax.psum_scatter(grads[0], "dp", scatter_dimension=1, tiled=True),
        lax.psum_scatter(grads[1], "dp", scatter_dimension=2, tiled=True),
        lax.psum_scatter(grads[2], "dp", scatter_dimension=1, tiled=True),
        lax.psum_scatter(grads[3], "dp", scatter_dimension=2, tiled=True),
        lax.psum_scatter(grads[4], "dp", scatter_dimension=2, tiled=True),
        lax.psum_scatter(grads[5], "dp", scatter_dimension=2, tiled=True),
        lax.psum_scatter(grads[6], "dp", scatter_dimension=2, tiled=True),
    )


def layer_forward(residual_stream, weights, segment, cosine, sine):
    qkv_w, dense_w, up_w, down_w, qkv_b, up_b, vec = weights
    heads = qkv_w.shape[1] // (3 * HD)
    vec_wide = vec.astype(jnp.float32)
    first_branch_input, second_in = norm_pair(residual_stream, vec_wide[:4])
    first_branch_input = first_branch_input.astype(jnp.bfloat16)
    second_in = second_in.astype(jnp.bfloat16)
    rows = first_branch_input.shape[0]
    mixed = jnp.dot(first_branch_input, qkv_w, preferred_element_type=jnp.float32) + qkv_b.reshape(
        -1
    ).astype(jnp.float32)
    mixed = mixed.reshape(rows, heads, 3, HD)
    query = rotate(mixed[:, :, 0], cosine, sine).astype(jnp.bfloat16)
    keys = rotate(mixed[:, :, 1], cosine, sine).astype(jnp.bfloat16)
    values = mixed[:, :, 2].astype(jnp.bfloat16)
    context, logsum = attention_forward(query, keys, values, segment)
    hidden = jnp.dot(second_in, up_w, preferred_element_type=jnp.float32) + up_b.reshape(-1).astype(
        jnp.float32
    )
    active = gelu_exact(hidden).astype(jnp.bfloat16)
    branch = jnp.dot(context, dense_w, preferred_element_type=jnp.float32) + jnp.dot(
        active, down_w, preferred_element_type=jnp.float32
    )
    branch = lax.psum(branch, "mp")
    result = residual_stream + branch + vec_wide[4] + vec_wide[5]
    return (
        result,
        (first_branch_input, second_in, query, keys, values, context, logsum, hidden, active),
    )


def layer_backward(residual_stream, weights, kept, grad_out, segment, cosine, sine):
    qkv_w, dense_w, up_w, down_w, qkv_b, up_b, vec = weights
    first_branch_input, second_in, query, keys, values, context, logsum, hidden, active = kept
    rows, heads = (query.shape[0], query.shape[1])
    grad_low = grad_out.astype(jnp.bfloat16)
    d_dense = jnp.dot(context.T, grad_low, preferred_element_type=jnp.float32)
    d_down = jnp.dot(active.T, grad_low, preferred_element_type=jnp.float32)
    d_context = (
        jnp.dot(grad_low, dense_w.T, preferred_element_type=jnp.float32)
        .astype(jnp.bfloat16)
        .reshape(rows, heads, HD)
    )
    d_active = jnp.dot(grad_low, down_w.T, preferred_element_type=jnp.float32)
    d_hidden = jax.vjp(gelu_exact, hidden)[1](d_active)[0].astype(jnp.bfloat16)
    d_up = jnp.dot(second_in.T, d_hidden, preferred_element_type=jnp.float32)
    d_up_bias = jnp.sum(d_hidden.astype(jnp.float32), axis=0)
    d_second = jnp.dot(d_hidden, up_w.T, preferred_element_type=jnp.float32)
    d_query, d_keys, d_values = attention_backward(query, keys, values, d_context, logsum, segment)
    d_mixed = jnp.stack(
        [rotate(d_query, cosine, -sine), rotate(d_keys, cosine, -sine), d_values], axis=2
    )
    d_mixed = d_mixed.reshape(rows, heads * 3 * HD).astype(jnp.bfloat16)
    d_qkv = jnp.dot(first_branch_input.T, d_mixed, preferred_element_type=jnp.float32)
    d_qkv_bias = jnp.sum(d_mixed.astype(jnp.float32), axis=0)
    d_first = jnp.dot(d_mixed, qkv_w.T, preferred_element_type=jnp.float32)
    vec_wide = vec.astype(jnp.float32)
    pullback = jax.vjp(norm_pair, residual_stream, vec_wide[:4])[1]
    d_resid, d_norm = pullback((d_first, d_second))
    d_resid, d_norm = lax.psum((d_resid, d_norm), "mp")
    d_out_bias = jnp.sum(grad_out, axis=0)
    d_vec = jnp.concatenate([d_norm, d_out_bias[None], d_out_bias[None]], axis=0)
    grads = (
        d_qkv,
        d_dense,
        d_up,
        d_down,
        d_qkv_bias.reshape(qkv_b.shape[0], -1),
        d_up_bias.reshape(up_b.shape[0], -1),
        d_vec,
    )
    return (grad_out + d_resid, grads)


def adam(weight, grad, first, second):
    first_new = beta_one * first + (1.0 - beta_one) * grad
    second_new = beta_two * second + (1.0 - beta_two) * grad * grad
    mean_hat = first_new / (1.0 - beta_one**ADAM_STEP)
    square_hat = second_new / (1.0 - beta_two**ADAM_STEP)
    old = weight.astype(jnp.float32)
    new_weight = old - rate * (mean_hat / (jnp.sqrt(square_hat) + adam_eps) + decay * old)
    return (grad, first_new, second_new, new_weight - old)


def body(
    tokens_in,
    cotangent,
    seq_lengths,
    qkv_weight,
    dense_weight,
    up_weight,
    down_weight,
    qkv_bias,
    up_bias,
    vectors,
    qkv_weight_first,
    dense_weight_first,
    up_weight_first,
    down_weight_first,
    qkv_bias_first,
    up_bias_first,
    vectors_first,
    qkv_weight_second,
    dense_weight_second,
    up_weight_second,
    down_weight_second,
    qkv_bias_second,
    up_bias_second,
    vectors_second,
):
    rows = tokens_in.shape[0]
    segment, position, valid = layout(seq_lengths[0], rows)
    cosine, sine = rotary_tables(position)
    shards = (qkv_weight, dense_weight, up_weight, down_weight, qkv_bias, up_bias, vectors)
    firsts = (
        qkv_weight_first,
        dense_weight_first,
        up_weight_first,
        down_weight_first,
        qkv_bias_first,
        up_bias_first,
        vectors_first,
    )
    seconds = (
        qkv_weight_second,
        dense_weight_second,
        up_weight_second,
        down_weight_second,
        qkv_bias_second,
        up_bias_second,
        vectors_second,
    )
    live = valid.astype(jnp.float32)[:, None]
    residual_stream = tokens_in.astype(jnp.float32)
    inputs, saved, fetched = ([], [], [])
    for layer in range(LAYERS):
        weights = fetch(shards, layer)
        inputs.append(residual_stream)
        residual_stream, kept = layer_forward(residual_stream, weights, segment, cosine, sine)
        saved.append(kept)
        fetched.append(weights)
    output = (residual_stream * live).astype(jnp.bfloat16)
    grad = cotangent.astype(jnp.float32) * live
    per_layer = [None] * LAYERS
    for layer in reversed(range(LAYERS)):
        weights = fetch(shards, layer)
        grad, grads = layer_backward(
            inputs[layer], weights, saved[layer], grad, segment, cosine, sine
        )
        per_layer[layer] = reduce_grads(tuple((item[None] for item in grads)))
    owned = tuple(
        (
            jnp.concatenate([per_layer[layer][slot] for layer in range(LAYERS)], axis=0)
            for slot in range(7)
        )
    )
    outs = [output, grad]
    for weight, summed, first, second in zip(shards, owned, firsts, seconds):
        outs.extend(adam(weight, summed, first, second))
    return tuple(outs)


def solution(mesh):
    placed = (
        P("dp", None),
        P("dp", None),
        P("dp", None),
        P(None, "dp", "mp"),
        P(None, "mp", "dp"),
        P(None, "dp", "mp"),
        P(None, "mp", "dp"),
        P(None, "mp", "dp"),
        P(None, "mp", "dp"),
        P(None, None, "dp"),
        P(None, "dp", "mp"),
        P(None, "mp", "dp"),
        P(None, "dp", "mp"),
        P(None, "mp", "dp"),
        P(None, "mp", "dp"),
        P(None, "mp", "dp"),
        P(None, None, "dp"),
        P(None, "dp", "mp"),
        P(None, "mp", "dp"),
        P(None, "dp", "mp"),
        P(None, "mp", "dp"),
        P(None, "mp", "dp"),
        P(None, "mp", "dp"),
        P(None, None, "dp"),
    )
    return jax.shard_map(
        body,
        mesh=mesh,
        in_specs=placed,
        out_specs=(
            P("dp", None),
            P("dp", None),
            P(None, "dp", "mp"),
            P(None, "dp", "mp"),
            P(None, "dp", "mp"),
            P(None, "dp", "mp"),
            P(None, "mp", "dp"),
            P(None, "mp", "dp"),
            P(None, "mp", "dp"),
            P(None, "mp", "dp"),
            P(None, "dp", "mp"),
            P(None, "dp", "mp"),
            P(None, "dp", "mp"),
            P(None, "dp", "mp"),
            P(None, "mp", "dp"),
            P(None, "mp", "dp"),
            P(None, "mp", "dp"),
            P(None, "mp", "dp"),
            P(None, "mp", "dp"),
            P(None, "mp", "dp"),
            P(None, "mp", "dp"),
            P(None, "mp", "dp"),
            P(None, "mp", "dp"),
            P(None, "mp", "dp"),
            P(None, "mp", "dp"),
            P(None, "mp", "dp"),
            P(None, None, "dp"),
            P(None, None, "dp"),
            P(None, None, "dp"),
            P(None, None, "dp"),
        ),
        check_vma=False,
    )
```

profile of v0, /device:TPU:0, one launch (start us, length us, event | category | flops | bytes accessed | tf_op | source)
XLA Modules:
  0.0 2900.1 jit_solution(7552632364524277170)
XLA Ops:
  115.0 31.7 %all-gather.27.cloned.1.call-done = bf16[1,2048,2048]{2,1,0:T(8,128)(2,1)} async-done(((bf16[1,256,2048]{2,1,0:T(8,128)(2,1)}), bf16[1,2048,2048]{2,1,0:T(8,128)(2,1)}) %all-gather.27.cloned.1.call-update) | async-done | bytes 8388624 | tf_op jit(solution)/shard_map/all_gather | solution.py:167
  146.7 33.9 %multiply_convert_fusion.4 = (bf16[1024,2048]{1,0:T(8,128)(2,1)}, f32[1024,2048]{1,0:T(8,128)}, f32[1024,2048]{1,0:T(8,128)}) fusion(f32[2048]{0:T(1024)S(1)} %bitcast_convert_fusion.2, bf16[1,2048,2048]{2,1,0:T(8,128)(2,1)} %all-gather.27.cloned.1.call-done, bf16[1024,2048]{1,0:T(8,128)(2,1)} %param.32, f32[2048]{0:T(1024)S(1)} %bitcast.349, ...), kind=kOutput, calls=%fused_computation.189 | convolution fusion | flops 8740929536 | bytes 33587200 | tf_op jit(solution)/shard_map/dot_general | solution.py:203
  180.5 24.4 all-gather.29.cloned.1.call-done
  257.5 272.0 %all-reduce.20.cloned.1.call-done = f32[1024,2048]{1,0:T(8,128)} async-done(((f32[1024,2048]{1,0:T(8,128)}), f32[1024,2048]{1,0:T(8,128)}) %all-reduce.20.cloned.1.call-update) | async-done | bytes 8388624 | tf_op jit(solution)/shard_map/psum | solution.py:210
  539.5 37.0 %all-gather.31.cloned.1.call-done = bf16[1,2048,1536]{2,1,0:T(8,128)(2,1)} async-done(((bf16[1,256,1536]{2,1,0:T(8,128)(2,1)}), bf16[1,2048,1536]{2,1,0:T(8,128)(2,1)}) %all-gather.31.cloned.1.call-update) | async-done | bytes 6291472 | tf_op jit(solution)/shard_map/all_gather | solution.py:165
  630.0 72.7 %while.54 = (s32[]{:T(128)}, f32[1536,2,256]{0,2,1:T(8,128)}, f32[1536,2,256]{0,2,1:T(8,128)}, f32[2,512,2,256]{1,0,3,2:T(2,128)}, s32[2]{0:T(128)S(1)}, /*index...) while((s32[]{:T(128)}, f32[1536,2,256]{0,2,1:T(8,128)}, ...), condition=%wide.region_20.21_spmd, body=%wide.region_18.20_spmd.sunk | while | flops 2703490560 | bytes 109115848 | solution.py:157
  723.4 33.7 %multiply_convert_fusion.3 = (bf16[1024,2048]{1,0:T(8,128)(2,1)}, f32[1024,2048]{1,0:T(8,128)}, f32[1024,2048]{1,0:T(8,128)}) fusion(f32[2048]{0:T(1024)S(1)} %copy-done.109, bf16[1,2048,2048]{2,1,0:T(8,128)(2,1)} %all-gather.35.cloned.1.call-done, f32[1024,2048]{1,0:T(8,128)} %copy-done.1, f32[2048]{0:T(1024)S(1)} %bitcast.353, f32[2048]{0:T(1024)S(1)} %bitcast.337, ...), kind=kOutput, calls=%fused_computation.173 | convolution fusion | flops 8738832384 | bytes 37781504 | tf_op jit(solution)/shard_map/dot_general | solution.py:203
  757.2 23.6 convert_reduce_fusion.1
  780.8 22.2 multiply_reduce_fusion.3
  835.6 272.7 %all-reduce.22.cloned.1.call-done = f32[1024,2048]{1,0:T(8,128)} async-done(((f32[1024,2048]{1,0:T(8,128)}), f32[1024,2048]{1,0:T(8,128)}) %all-reduce.22.cloned.1.call-update) | async-done | bytes 8388624 | tf_op jit(solution)/shard_map/psum | solution.py:246
  1121.3 70.4 %while.55 = (s32[]{:T(128)}, f32[1536,2,256]{0,2,1:T(8,128)}, f32[1536,2,256]{2,0,1:T(8,128)}, f32[2,512,2,256]{3,1,0,2:T(8,128)}, s32[2]{0:T(128)S(1)}, /*index...) while((s32[]{:T(128)}, f32[1536,2,256]{0,2,1:T(8,128)}, ...), condition=%wide.region_26.27_spmd, body=%wide.region_24.26_spmd.sunk | while | flops 2703490560 | bytes 98629992 | solution.py:157
  1298.7 542.4 %all-reduce.26.cloned.1.call-done = (f32[1024,2048]{1,0:T(8,128)}, f32[1024,2048]{1,0:T(8,128)}) async-done(((f32[1024,2048]{1,0:T(8,128)}, f32[1024,2048]{1,0:T(8,128)}), (f32[1024,2048]{1,0:T(8,128)}, f32[1024,2048]{1,0:T(8,128)})) %all-reduce.26.cloned.1.call-update) | async-done | bytes 16777232 | tf_op jit(solution)/shard_map/psum | solution.py:210
  1841.1 19.8 fusion.117
  1990.7 33.4 %reduce-scatter.47.cloned.1.call-done = f32[16,16]{1,0:T(8,128)} async-done(((f32[128,16]{1,0:T(8,128)}), f32[16,16]{1,0:T(8,128)}) %reduce-scatter.47.cloned.1.call-update) | async-done | bytes 1040
  2025.6 54.1 %reduce-scatter.27.cloned.1.call-done = f32[1,512,256]{2,1,0:T(8,128)} async-done(((f32[1,512,2048]{2,1,0:T(8,128)}), f32[1,512,256]{2,1,0:T(8,128)}) %reduce-scatter.27.cloned.1.call-update) | async-done | bytes 524304 | tf_op jit(solution)/shard_map/reduce_scatter | solution.py:178
  2080.8 54.0 %reduce-scatter.29.cloned.1.call-done = f32[1,512,256]{2,1,0:T(8,128)} async-done(((f32[1,512,2048]{2,1,0:T(8,128)}), f32[1,512,256]{2,1,0:T(8,128)}) %reduce-scatter.29.cloned.1.call-update) | async-done | bytes 524304 | tf_op jit(solution)/shard_map/reduce_scatter | solution.py:178
  2139.7 32.2 %reduce-scatter.39.cloned.1.call-done = f32[1,6,256]{2,1,0:T(8,128)} async-done(((f32[1,6,2048]{2,1,0:T(8,128)}), f32[1,6,256]{2,1,0:T(8,128)}) %reduce-scatter.39.cloned.1.call-update) | async-done | bytes 6160 | tf_op jit(solution)/shard_map/reduce_scatter | solution.py:183
  2172.6 36.0 %reduce-scatter.41.cloned.1.call-done = f32[1,6,256]{2,1,0:T(8,128)} async-done(((f32[1,6,2048]{2,1,0:T(8,128)}), f32[1,6,256]{2,1,0:T(8,128)}) %reduce-scatter.41.cloned.1.call-update) | async-done | bytes 6160 | tf_op jit(solution)/shard_map/reduce_scatter | solution.py:183
  2211.8 93.2 %reduce-scatter.23.cloned.1.call-done = f32[1,256,1536]{2,1,0:T(8,128)} async-done(((f32[1,2048,1536]{2,1,0:T(8,128)}), f32[1,256,1536]{2,1,0:T(8,128)}) %reduce-scatter.23.cloned.1.call-update) | async-done | bytes 1572880 | tf_op jit(solution)/shard_map/reduce_scatter | solution.py:177
  2306.5 94.8 %reduce-scatter.25.cloned.1.call-done = f32[1,256,1536]{2,1,0:T(8,128)} async-done(((f32[1,2048,1536]{2,1,0:T(8,128)}), f32[1,256,1536]{2,1,0:T(8,128)}) %reduce-scatter.25.cloned.1.call-update) | async-done | bytes 1572880 | tf_op jit(solution)/shard_map/reduce_scatter | solution.py:177
  2410.8 110.5 %reduce-scatter.31.cloned.1.call-done = f32[1,256,2048]{2,1,0:T(8,128)} async-done(((f32[1,2048,2048]{2,1,0:T(8,128)}), f32[1,256,2048]{2,1,0:T(8,128)}) %reduce-scatter.31.cloned.1.call-update) | async-done | bytes 2097168 | tf_op jit(solution)/shard_map/reduce_scatter | solution.py:179
  2524.4 116.7 %reduce-scatter.35.cloned.1.call-done = f32[1,2048,256]{2,1,0:T(8,128)} async-done(((f32[1,2048,2048]{2,1,0:T(8,128)}), f32[1,2048,256]{2,1,0:T(8,128)}) %reduce-scatter.35.cloned.1.call-update) | async-done | bytes 2097168 | tf_op jit(solution)/shard_map/reduce_scatter | solution.py:180
  2644.1 116.9 %reduce-scatter.33.cloned.1.call-done = f32[1,256,2048]{2,1,0:T(8,128)} async-done(((f32[1,2048,2048]{2,1,0:T(8,128)}), f32[1,256,2048]{2,1,0:T(8,128)}) %reduce-scatter.33.cloned.1.call-update) | async-done | bytes 2097168 | tf_op jit(solution)/shard_map/reduce_scatter | solution.py:179
  2773.1 107.8 %reduce-scatter.37.cloned.1.call-done = f32[1,2048,256]{2,1,0:T(8,128)} async-done(((f32[1,2048,2048]{2,1,0:T(8,128)}), f32[1,2048,256]{2,1,0:T(8,128)}) %reduce-scatter.37.cloned.1.call-update) | async-done | bytes 2097168 | tf_op jit(solution)/shard_map/reduce_scatter | solution.py:180
  (616 shorter events, 751.2 us)
Async XLA Ops:
  11.0 135.7 %all-gather.27.cloned.1.call-start = ((), (), s32[]{:S(2)}) async-start(), calls=%async_computation.28 | async-start | bytes 9437184 | tf_op jit(solution)/shard_map/all_gather | solution.py:167
  12.5 192.4 %all-gather.29.cloned.1.call-start = ((), (), s32[]{:S(2)}) async-start(), calls=%async_computation.29 | async-start | bytes 9437184 | tf_op jit(solution)/shard_map/all_gather | solution.py:168
  15.6 235.6 %all-gather.33.cloned.1.call-start = ((), (), s32[]{:S(2)}) async-start(), calls=%async_computation.31 | async-start | bytes 2359296 | tf_op jit(solution)/shard_map/all_gather | solution.py:166
  16.2 513.3 %all-reduce.20.cloned.1.call-start = ((), (), s32[]{:S(2)}) async-start(), calls=%async_computation.14 | async-start | bytes 16777216 | tf_op jit(solution)/shard_map/psum | solution.py:210
  220.7 355.8 %all-gather.31.cloned.1.call-start = ((), (), s32[]{:S(2)}) async-start(), calls=%async_computation.30 | async-start | bytes 7077888 | tf_op jit(solution)/shard_map/all_gather | solution.py:165
  221.4 501.9 %all-gather.35.cloned.1.call-start = ((), (), s32[]{:S(2)}) async-start(), calls=%async_computation.32 | async-start | bytes 9437184 | tf_op jit(solution)/shard_map/all_gather | solution.py:167
  222.2 535.0 %all-gather.37.cloned.1.call-start = ((), (), s32[]{:S(2)}) async-start(), calls=%async_computation.33 | async-start | bytes 9437184 | tf_op jit(solution)/shard_map/all_gather | solution.py:168
  222.9 885.3 %all-reduce.22.cloned.1.call-start = ((), (), s32[]{:S(2)}) async-start(), calls=%async_computation.15 | async-start | bytes 16777216 | tf_op jit(solution)/shard_map/psum | solution.py:246
  817.2 1023.8 %all-reduce.26.cloned.1.call-start = ((), (), s32[]{:S(2)}) async-start(), calls=%async_computation.39 | async-start | bytes 33554432 | tf_op jit(solution)/shard_map/psum | solution.py:210
  1278.6 598.3 %all-reduce.24.cloned.1.call-start = ((), (), s32[]{:S(2)}) async-start(), calls=%async_computation.38 | async-start | bytes 131072 | tf_op jit(solution)/shard_map/psum | solution.py:246
  1280.6 695.3 %reduce-scatter.45.cloned.1.call-start = ((), (), s32[]{:S(2)}) async-start(), calls=%async_computation.35 | async-start | bytes 73728
  1281.5 695.4 %reduce-scatter.49.cloned.1.call-start = ((), (), s32[]{:S(2)}) async-start(), calls=%async_computation.37 | async-start | bytes 73728
  1282.3 705.2 %reduce-scatter.43.cloned.1.call-start = ((), (), s32[]{:S(2)}) async-start(), calls=%async_computation.34 | async-start | bytes 73728
  1283.1 741.0 %reduce-scatter.47.cloned.1.call-start = ((), (), s32[]{:S(2)}) async-start(), calls=%async_computation.36 | async-start | bytes 73728
  1283.9 795.7 %reduce-scatter.27.cloned.1.call-start = ((), (), s32[]{:S(2)}) async-start(), calls=%async_computation.18 | async-start | bytes 4718592 | tf_op jit(solution)/shard_map/reduce_scatter | solution.py:178
  1290.7 844.1 %reduce-scatter.29.cloned.1.call-start = ((), (), s32[]{:S(2)}) async-start(), calls=%async_computation.19 | async-start | bytes 4718592 | tf_op jit(solution)/shard_map/reduce_scatter | solution.py:178
  1298.7 873.3 %reduce-scatter.39.cloned.1.call-start = ((), (), s32[]{:S(2)}) async-start(), calls=%async_computation.24 | async-start | bytes 73728 | tf_op jit(solution)/shard_map/reduce_scatter | solution.py:183
  1878.4 330.2 %reduce-scatter.41.cloned.1.call-start = ((), (), s32[]{:S(2)}) async-start(), calls=%async_computation.25 | async-start | bytes 73728 | tf_op jit(solution)/shard_map/reduce_scatter | solution.py:183
  1879.9 425.1 %reduce-scatter.23.cloned.1.call-start = ((), (), s32[]{:S(2)}) async-start(), calls=%async_computation.16 | async-start | bytes 14155776 | tf_op jit(solution)/shard_map/reduce_scatter | solution.py:177
  1894.0 507.3 %reduce-scatter.25.cloned.1.call-start = ((), (), s32[]{:S(2)}) async-start(), calls=%async_computation.17 | async-start | bytes 14155776 | tf_op jit(solution)/shard_map/reduce_scatter | solution.py:177
  1910.7 610.6 %reduce-scatter.31.cloned.1.call-start = ((), (), s32[]{:S(2)}) async-start(), calls=%async_computation.20 | async-start | bytes 18874368 | tf_op jit(solution)/shard_map/reduce_scatter | solution.py:179
  1927.2 713.9 %reduce-scatter.35.cloned.1.call-start = ((), (), s32[]{:S(2)}) async-start(), calls=%async_computation.22 | async-start | bytes 18874368 | tf_op jit(solution)/shard_map/reduce_scatter | solution.py:180
  1942.8 818.2 %reduce-scatter.33.cloned.1.call-start = ((), (), s32[]{:S(2)}) async-start(), calls=%async_computation.21 | async-start | bytes 18874368 | tf_op jit(solution)/shard_map/reduce_scatter | solution.py:179
  1959.9 921.0 %reduce-scatter.37.cloned.1.call-start = ((), (), s32[]{:S(2)}) async-start(), calls=%async_computation.23 | async-start | bytes 18874368 | tf_op jit(solution)/shard_map/reduce_scatter | solution.py:180
  (130 other events, 5526.5 us)
Sparse Core Ops, SparseCore 0:
  10.5 48.5 all-gather.22
  92.2 54.3 all-gather.26
  149.0 55.9 all-gather.28
  238.6 290.8 all-reduce.19
  531.9 44.5 all-gather.30
  579.0 54.3 all-gather.34
  635.9 55.9 all-gather.36
  817.4 290.8 all-reduce.21
  1278.8 562.2 all-reduce.25
  1843.9 33.0 all-reduce.23
  1880.8 32.8 reduce-scatter.44
  1917.2 33.2 reduce-scatter.48
  1954.2 33.2 reduce-scatter.42
  1990.9 33.2 reduce-scatter.46
  2028.3 51.3 reduce-scatter.26
  2083.5 51.3 reduce-scatter.28
  2138.7 33.2 reduce-scatter.38
  2175.3 33.2 reduce-scatter.40
  2212.5 92.4 reduce-scatter.22
  2308.9 92.3 reduce-scatter.24
  2405.3 115.9 reduce-scatter.30
  2525.1 115.9 reduce-scatter.34
  2645.1 115.9 reduce-scatter.32
  2764.9 115.9 reduce-scatter.36
  (2 shorter events, 56.5 us)
where the time goes:
time: 2910 us; the launch traced here: 2900 us
  waiting for transfers between devices  2060 us (71%)
  matrix products  430 us (15%)
  local copies, waits for them, and re-layouts  204 us (7%)
  other arithmetic  123 us (4%)
  blocking collectives  55.7 us (2%)
    psum x2, waiting for transfers between devices, layer_forward(): branch = lax.psum(branch, 'mp')  814 us
    psum x2, waiting for transfers between devices, layer_backward(): d_resid, d_norm = lax.psum((d_resid, d_norm), 'mp')  289 us
    reduce_scatter x2, waiting for transfers between devices, reduce_grads(): lax.psum_scatter(grads[2], 'dp', scatter_dimension=1, tiled=True)  227 us
    reduce_scatter x2, waiting for transfers between devices, reduce_grads(): lax.psum_scatter(grads[3], 'dp', scatter_dimension=2, tiled=True)  224 us
    reduce_scatter x2, waiting for transfers between devices, reduce_grads(): lax.psum_scatter(grads[0], 'dp', scatter_dimension=1, tiled=True)  188 us
    reduce_scatter x2, waiting for transfers between devices, reduce_grads(): lax.psum_scatter(grads[1], 'dp', scatter_dimension=2, tiled=True)  108 us
    reduce_scatter x2, waiting for transfers between devices, reduce_grads(): lax.psum_scatter(grads[6], 'dp', scatter_dimension=2, tiled=True)  68.2 us
    dot_general x2, matrix products, layer_forward(): jnp.dot(second_in, up_w, preferred_element_type=jnp.float32)  67.6 us
  transfers between devices with their start and end apart: 26, of which 20 were waited for; matrix products, arithmetic and copies ran while one was open for 17% of the time, Pallas kernels for 0%

commit v1 on v0

--- a/solution.py
+++ b/solution.py
@@ -207,7 +207,7 @@
     branch = jnp.dot(context, dense_w, preferred_element_type=jnp.float32) + jnp.dot(
         active, down_w, preferred_element_type=jnp.float32
     )
-    branch = lax.psum(branch, "mp")
+    branch = jnp.sum(lax.all_gather(branch, "mp"), axis=0)
     result = residual_stream + branch + vec_wide[4] + vec_wide[5]
     return (
         result,

time: 2910 us -> 3410 us (1.17)
  waiting for transfers between devices: 2060 us -> 2530 us
  other arithmetic: 123 us -> 158 us
    all_gather x0 -> x2, waiting for transfers between devices: none -> 946 us  [layer_forward(): branch = jnp.sum(lax.all_gather(branch, 'mp'), axis=0)]
    psum x2 -> x0, waiting for transfers between devices: 814 us -> none  [layer_forward(): branch = lax.psum(branch, 'mp')]
    psum x2 -> x3, waiting for transfers between devices: 289 us -> 584 us  [layer_backward(): d_resid, d_norm = lax.psum((d_resid, d_norm), 'mp')]
  transfers between devices with their start and end apart: 26 -> 27, of which waited for: 20 -> 23; matrix products, arithmetic and copies ran while one was open for 17% -> 15% of each run, Pallas kernels for 0% -> 0%
where the time goes in v1:
time: 3410 us; the launch traced here: 3400 us
  waiting for transfers between devices  2530 us (74%)
  matrix products  433 us (13%)
  local copies, waits for them, and re-layouts  205 us (6%)
  other arithmetic  158 us (5%)
  blocking collectives  55.7 us (2%)
    all_gather x2, waiting for transfers between devices, layer_forward(): branch = jnp.sum(lax.all_gather(branch, 'mp'), axis=0)  946 us
    psum x3, waiting for transfers between devices, layer_backward(): d_resid, d_norm = lax.psum((d_resid, d_norm), 'mp')  584 us
    reduce_scatter x2, waiting for transfers between devices, reduce_grads(): lax.psum_scatter(grads[2], 'dp', scatter_dimension=1, tiled=True)  227 us
    reduce_scatter x2, waiting for transfers between devices, reduce_grads(): lax.psum_scatter(grads[3], 'dp', scatter_dimension=2, tiled=True)  225 us
    reduce_scatter x2, waiting for transfers between devices, reduce_grads(): lax.psum_scatter(grads[0], 'dp', scatter_dimension=1, tiled=True)  188 us
    reduce_scatter x2, waiting for transfers between devices, reduce_grads(): lax.psum_scatter(grads[1], 'dp', scatter_dimension=2, tiled=True)  108 us
  transfers between devices with their start and end apart: 27, of which 23 were waited for; matrix products, arithmetic and copies ran while one was open for 15% of the time, Pallas kernels for 0%

profile of v1, /device:TPU:0, one launch (start us, length us, event | category | flops | bytes accessed | tf_op | source)
XLA Modules:
  0.0 3401.4 jit_solution(15533033443977941767)
XLA Ops:
  115.3 31.4 all-gather.31.cloned.1.call-done
  146.7 33.6 multiply_convert_fusion.4
  180.3 24.7 all-gather.33.cloned.1.call-done
  251.4 530.9 %all-gather.35.cloned.1.call-done = f32[4096,2048]{1,0:T(8,128)} async-done(((f32[1024,2048]{1,0:T(8,128)}), f32[4096,2048]{1,0:T(8,128)}) %all-gather.35.cloned.1.call-update) | async-done | bytes 33554448 | tf_op jit(solution)/shard_map/all_gather | solution.py:210
  887.3 28.6 all-gather.41.cloned.1.call-done
  915.9 34.0 multiply_convert_fusion.3
  949.9 24.5 all-gather.43.cloned.1.call-done
  1002.0 73.4 %while.54 = (s32[]{:T(128)}, f32[1536,2,256]{0,2,1:T(8,128)}, f32[1536,2,256]{0,2,1:T(8,128)}, f32[2,512,2,256]{1,0,3,2:T(2,128)}, s32[2]{0:T(128)S(1)}, /*index...) while((s32[]{:T(128)}, f32[1536,2,256]{0,2,1:T(8,128)}, ...), condition=%wide.region_20.21_spmd, body=%wide.region_18.20_spmd.sunk | while | flops 2703490560 | bytes 109115848 | solution.py:157
  1136.5 415.0 %all-gather.45.cloned.1.call-done = f32[4096,2048]{1,0:T(8,128)} async-done(((f32[1024,2048]{1,0:T(8,128)}), f32[4096,2048]{1,0:T(8,128)}) %all-gather.45.cloned.1.call-update) | async-done | bytes 33554448 | tf_op jit(solution)/shard_map/all_gather | solution.py:210
  1593.1 289.1 %all-reduce.18.cloned.1.call-done = f32[1024,2048]{1,0:T(8,128)} async-done(((f32[1024,2048]{1,0:T(8,128)}), f32[1024,2048]{1,0:T(8,128)}) %all-reduce.18.cloned.1.call-update) | async-done | bytes 8388624 | tf_op jit(solution)/shard_map/psum | solution.py:246
  1895.1 70.2 %while.55 = (s32[]{:T(128)}, f32[1536,2,256]{0,2,1:T(8,128)}, f32[1536,2,256]{2,0,1:T(8,128)}, f32[2,512,2,256]{3,1,0,2:T(8,128)}, s32[2]{0:T(128)S(1)}, /*index...) while((s32[]{:T(128)}, f32[1536,2,256]{0,2,1:T(8,128)}, ...), condition=%wide.region_26.27_spmd, body=%wide.region_24.26_spmd.sunk | while | flops 2703490560 | bytes 98629992 | solution.py:157
  2072.4 270.0 %all-reduce.20.cloned.1.call-done = f32[1024,2048]{1,0:T(8,128)} async-done(((f32[1024,2048]{1,0:T(8,128)}), f32[1024,2048]{1,0:T(8,128)}) %all-reduce.20.cloned.1.call-update) | async-done | bytes 8388624 | tf_op jit(solution)/shard_map/psum | solution.py:246
  2353.9 24.6 all-reduce.22.cloned.1.call-done
  2492.0 33.4 reduce-scatter.47.cloned.1.call-done
  2526.9 54.1 %reduce-scatter.27.cloned.1.call-done = f32[1,512,256]{2,1,0:T(8,128)} async-done(((f32[1,512,2048]{2,1,0:T(8,128)}), f32[1,512,256]{2,1,0:T(8,128)}) %reduce-scatter.27.cloned.1.call-update) | async-done | bytes 524304 | tf_op jit(solution)/shard_map/reduce_scatter | solution.py:178
  2582.1 54.2 %reduce-scatter.29.cloned.1.call-done = f32[1,512,256]{2,1,0:T(8,128)} async-done(((f32[1,512,2048]{2,1,0:T(8,128)}), f32[1,512,256]{2,1,0:T(8,128)}) %reduce-scatter.29.cloned.1.call-update) | async-done | bytes 524304 | tf_op jit(solution)/shard_map/reduce_scatter | solution.py:178
  2641.2 32.0 reduce-scatter.39.cloned.1.call-done
  2673.9 36.1 %reduce-scatter.41.cloned.1.call-done = f32[1,6,256]{2,1,0:T(8,128)} async-done(((f32[1,6,2048]{2,1,0:T(8,128)}), f32[1,6,256]{2,1,0:T(8,128)}) %reduce-scatter.41.cloned.1.call-update) | async-done | bytes 6160 | tf_op jit(solution)/shard_map/reduce_scatter | solution.py:183
  2713.2 93.2 %reduce-scatter.23.cloned.1.call-done = f32[1,256,1536]{2,1,0:T(8,128)} async-done(((f32[1,2048,1536]{2,1,0:T(8,128)}), f32[1,256,1536]{2,1,0:T(8,128)}) %reduce-scatter.23.cloned.1.call-update) | async-done | bytes 1572880 | tf_op jit(solution)/shard_map/reduce_scatter | solution.py:177
  2807.9 94.8 %reduce-scatter.25.cloned.1.call-done = f32[1,256,1536]{2,1,0:T(8,128)} async-done(((f32[1,2048,1536]{2,1,0:T(8,128)}), f32[1,256,1536]{2,1,0:T(8,128)}) %reduce-scatter.25.cloned.1.call-update) | async-done | bytes 1572880 | tf_op jit(solution)/shard_map/reduce_scatter | solution.py:177
  2912.2 110.3 %reduce-scatter.31.cloned.1.call-done = f32[1,256,2048]{2,1,0:T(8,128)} async-done(((f32[1,2048,2048]{2,1,0:T(8,128)}), f32[1,256,2048]{2,1,0:T(8,128)}) %reduce-scatter.31.cloned.1.call-update) | async-done | bytes 2097168 | tf_op jit(solution)/shard_map/reduce_scatter | solution.py:179
  3025.7 116.8 %reduce-scatter.35.cloned.1.call-done = f32[1,2048,256]{2,1,0:T(8,128)} async-done(((f32[1,2048,2048]{2,1,0:T(8,128)}), f32[1,2048,256]{2,1,0:T(8,128)}) %reduce-scatter.35.cloned.1.call-update) | async-done | bytes 2097168 | tf_op jit(solution)/shard_map/reduce_scatter | solution.py:180
  3145.5 116.8 %reduce-scatter.33.cloned.1.call-done = f32[1,256,2048]{2,1,0:T(8,128)} async-done(((f32[1,2048,2048]{2,1,0:T(8,128)}), f32[1,256,2048]{2,1,0:T(8,128)}) %reduce-scatter.33.cloned.1.call-update) | async-done | bytes 2097168 | tf_op jit(solution)/shard_map/reduce_scatter | solution.py:179
  3274.4 107.8 %reduce-scatter.37.cloned.1.call-done = f32[1,2048,256]{2,1,0:T(8,128)} async-done(((f32[1,2048,2048]{2,1,0:T(8,128)}), f32[1,2048,256]{2,1,0:T(8,128)}) %reduce-scatter.37.cloned.1.call-update) | async-done | bytes 2097168 | tf_op jit(solution)/shard_map/reduce_scatter | solution.py:180
  (595 shorter events, 860.0 us)
Async XLA Ops:
  12.5 192.5 %all-gather.33.cloned.1.call-start = ((), (), s32[]{:S(2)}) async-start(), calls=%async_computation.29 | async-start | bytes 9437184 | tf_op jit(solution)/shard_map/all_gather | solution.py:168
  15.6 766.7 %all-gather.35.cloned.1.call-start = ((), (), s32[]{:S(2)}) async-start(), calls=%async_computation.30 | async-start | bytes 41943040 | tf_op jit(solution)/shard_map/all_gather | solution.py:210
  220.7 607.6 %all-gather.37.cloned.1.call-start = ((), (), s32[]{:S(2)}) async-start(), calls=%async_computation.31 | async-start | bytes 7077888 | tf_op jit(solution)/shard_map/all_gather | solution.py:165
  221.3 658.3 %all-gather.39.cloned.1.call-start = ((), (), s32[]{:S(2)}) async-start(), calls=%async_computation.32 | async-start | bytes 2359296 | tf_op jit(solution)/shard_map/all_gather | solution.py:166
  222.1 693.8 %all-gather.41.cloned.1.call-start = ((), (), s32[]{:S(2)}) async-start(), calls=%async_computation.33 | async-start | bytes 9437184 | tf_op jit(solution)/shard_map/all_gather | solution.py:167
  222.8 751.5 %all-gather.43.cloned.1.call-start = ((), (), s32[]{:S(2)}) async-start(), calls=%async_computation.34 | async-start | bytes 9437184 | tf_op jit(solution)/shard_map/all_gather | solution.py:168
  223.5 1328.0 %all-gather.45.cloned.1.call-start = ((), (), s32[]{:S(2)}) async-start(), calls=%async_computation.35 | async-start | bytes 41943040 | tf_op jit(solution)/shard_map/all_gather | solution.py:210
  990.0 892.3 %all-reduce.18.cloned.1.call-start = ((), (), s32[]{:S(2)}) async-start(), calls=%async_computation.14 | async-start | bytes 16777216 | tf_op jit(solution)/shard_map/psum | solution.py:246
  1593.1 749.4 %all-reduce.20.cloned.1.call-start = ((), (), s32[]{:S(2)}) async-start(), calls=%async_computation.15 | async-start | bytes 16777216 | tf_op jit(solution)/shard_map/psum | solution.py:246
  2052.4 326.0 %all-reduce.22.cloned.1.call-start = ((), (), s32[]{:S(2)}) async-start(), calls=%async_computation.40 | async-start | bytes 131072 | tf_op jit(solution)/shard_map/psum | solution.py:246
  2054.4 422.7 %reduce-scatter.45.cloned.1.call-start = ((), (), s32[]{:S(2)}) async-start(), calls=%async_computation.37 | async-start | bytes 73728
  2055.3 422.7 %reduce-scatter.49.cloned.1.call-start = ((), (), s32[]{:S(2)}) async-start(), calls=%async_computation.39 | async-start | bytes 73728
  2056.1 432.7 %reduce-scatter.43.cloned.1.call-start = ((), (), s32[]{:S(2)}) async-start(), calls=%async_computation.36 | async-start | bytes 73728
  2056.9 468.5 %reduce-scatter.47.cloned.1.call-start = ((), (), s32[]{:S(2)}) async-start(), calls=%async_computation.38 | async-start | bytes 73728
  2057.7 523.3 %reduce-scatter.27.cloned.1.call-start = ((), (), s32[]{:S(2)}) async-start(), calls=%async_computation.18 | async-start | bytes 4718592 | tf_op jit(solution)/shard_map/reduce_scatter | solution.py:178
  2064.4 571.9 %reduce-scatter.29.cloned.1.call-start = ((), (), s32[]{:S(2)}) async-start(), calls=%async_computation.19 | async-start | bytes 4718592 | tf_op jit(solution)/shard_map/reduce_scatter | solution.py:178
  2072.4 600.8 %reduce-scatter.39.cloned.1.call-start = ((), (), s32[]{:S(2)}) async-start(), calls=%async_computation.24 | async-start | bytes 73728 | tf_op jit(solution)/shard_map/reduce_scatter | solution.py:183
  2379.9 330.2 %reduce-scatter.41.cloned.1.call-start = ((), (), s32[]{:S(2)}) async-start(), calls=%async_computation.25 | async-start | bytes 73728 | tf_op jit(solution)/shard_map/reduce_scatter | solution.py:183
  2381.4 425.0 %reduce-scatter.23.cloned.1.call-start = ((), (), s32[]{:S(2)}) async-start(), calls=%async_computation.16 | async-start | bytes 14155776 | tf_op jit(solution)/shard_map/reduce_scatter | solution.py:177
  2395.5 507.3 %reduce-scatter.25.cloned.1.call-start = ((), (), s32[]{:S(2)}) async-start(), calls=%async_computation.17 | async-start | bytes 14155776 | tf_op jit(solution)/shard_map/reduce_scatter | solution.py:177
  2412.2 610.4 %reduce-scatter.31.cloned.1.call-start = ((), (), s32[]{:S(2)}) async-start(), calls=%async_computation.20 | async-start | bytes 18874368 | tf_op jit(solution)/shard_map/reduce_scatter | solution.py:179
  2428.7 713.8 %reduce-scatter.35.cloned.1.call-start = ((), (), s32[]{:S(2)}) async-start(), calls=%async_computation.22 | async-start | bytes 18874368 | tf_op jit(solution)/shard_map/reduce_scatter | solution.py:180
  2444.1 818.2 %reduce-scatter.33.cloned.1.call-start = ((), (), s32[]{:S(2)}) async-start(), calls=%async_computation.21 | async-start | bytes 18874368 | tf_op jit(solution)/shard_map/reduce_scatter | solution.py:179
  2461.3 920.9 %reduce-scatter.37.cloned.1.call-start = ((), (), s32[]{:S(2)}) async-start(), calls=%async_computation.23 | async-start | bytes 18874368 | tf_op jit(solution)/shard_map/reduce_scatter | solution.py:180
  (118 other events, 9342.8 us)
Sparse Core Ops, SparseCore 0:
  10.5 48.5 all-gather.26
  92.3 54.4 all-gather.30
  149.0 55.9 all-gather.32
  220.8 561.3 all-gather.34
  784.6 43.7 all-gather.36
  861.5 54.3 all-gather.40
  918.4 55.9 all-gather.42
  990.1 561.3 all-gather.44
  1593.2 289.0 all-reduce.17
  2052.5 289.8 all-reduce.19
  2345.3 33.0 all-reduce.21
  2418.5 33.2 reduce-scatter.48
  2455.5 33.2 reduce-scatter.42
  2492.2 33.2 reduce-scatter.46
  2529.6 51.3 reduce-scatter.26
  2584.9 51.3 reduce-scatter.28
  2640.0 33.2 reduce-scatter.38
  2676.8 33.2 reduce-scatter.40
  2713.9 92.4 reduce-scatter.22
  2810.3 92.3 reduce-scatter.24
  2906.6 115.9 reduce-scatter.30
  3026.5 115.9 reduce-scatter.34
  3146.3 115.9 reduce-scatter.32
  3266.2 115.9 reduce-scatter.36
  (3 shorter events, 89.1 us)
